TPU v7x, 32 devices: a whole 2x2x4 slice. The times are simulated.
32 devices in a mesh: inl: 4 (over x, core), xl: 8 (over z, y).
Axes of the slice: x: 2, y: 2, z: 4, core: 2. Of those that a mesh axis runs over, the one named last changes fastest.
Arguments:
- baseline: float32 [16, 128, 1024], P('inl', 'xl'), may hold values from -600 to 600
- monitor: float32 [16, 128, 1024], P('inl', 'xl'), may hold values from -900 to 900
- shift_model: float32 [4, 32, 128], P(None, None, 'xl'), may hold values from -4 to 4
- knot_start: int32 [32, 4], replicated, may hold values from -12 to 13, as said below
- half_width: int32 [8], P('xl'), may hold values from 1 to 3
Outputs:
- shift_obs: float32 [16, 128, 1024], P('inl', 'xl')
- delta: float32 [4, 32, 128], P(None, 'xl', 'inl')
Inputs may be any that keep to these rules, and one draw needn't show every extreme that they name: `knot_start`: basis function k of a window starts at sample k * 8 - 3 * 4 or one later, relative to the window's first sample.
All inputs are finite; a program needn't handle non-finite values.
Results may differ from a plain program's by a relative error of at most 0.00018.
Values sent between devices are 32-bit elements; how exact they have to be, the bound alone decides.
A program may use at most 64 MiB of HBM per device.

v0:
```python
import jax
import jax.numpy as jnp
from jax import lax
from jax.sharding import PartitionSpec as P

LAGS = 15
TWIN = 12
HMAX = 3
WINLEN = 32
KW = 4
KSTEP = 8
EPSILON = 1e-06
SHARPNESS = 6.0
DAMPING = 0.5


def extended(block, sides, width):
    for axis, dim in sides:
        count = lax.axis_size(axis)
        forward = [(i, i + 1) for i in range(count - 1)]
        backward = [(target, source) for source, target in forward]
        low = lax.ppermute(
            lax.slice_in_dim(block, block.shape[dim] - width, None, axis=dim), axis, forward
        )
        high = lax.ppermute(lax.slice_in_dim(block, 0, width, axis=dim), axis, backward)
        block = jnp.concatenate([low, block, high], axis=dim)
    return block


def spline(offset):
    square = offset * offset
    cubed = square * offset
    piece_one = cubed / 6.0
    piece_two = (-3.0 * cubed + 12.0 * square - 12.0 * offset + 4.0) / 6.0
    piece_three = (3.0 * cubed - 24.0 * square + 60.0 * offset - 44.0) / 6.0
    remain = 4.0 - offset
    piece_four = remain * remain * remain / 6.0
    result = jnp.where(offset < 4.0, piece_four, 0.0 * offset)
    result = jnp.where(offset < 3.0, piece_three, result)
    result = jnp.where(offset < 2.0, piece_two, result)
    result = jnp.where(offset < 1.0, piece_one, result)
    return jnp.where(offset < 0.0, 0.0 * offset, result)


def basis_table(knot_start):
    positions = jnp.arange(WINLEN).astype(jnp.float32)
    offset = (positions[None, None, :] - knot_start[:, :, None].astype(jnp.float32)) / KSTEP
    return spline(offset)


def solve_small(matrix, target):
    lower = [[None] * KW for _ in range(KW)]
    for column in range(KW):
        pivot = matrix[column][column]
        for inner in range(column):
            pivot = pivot - lower[column][inner] * lower[column][inner]
        lower[column][column] = jnp.sqrt(pivot)
        for target_row in range(column + 1, KW):
            entry = matrix[target_row][column]
            for inner in range(column):
                entry = entry - lower[target_row][inner] * lower[column][inner]
            lower[target_row][column] = entry / lower[column][column]
    forward = []
    for column in range(KW):
        entry = target[column]
        for inner in range(column):
            entry = entry - lower[column][inner] * forward[inner]
        forward.append(entry / lower[column][column])
    backward = [None] * KW
    for column in range(KW - 1, -1, -1):
        entry = forward[column]
        for inner in range(column + 1, KW):
            entry = entry - lower[inner][column] * backward[inner]
        backward[column] = entry / lower[column][column]
    return jnp.stack(backward)


def box_time(values):
    samples = values.shape[2]
    width = 2 * TWIN + 1
    padded = jnp.pad(values, ((0, 0), (0, 0), (TWIN, TWIN)))
    partial_sums = {1: padded}
    length = 1
    while 2 * length <= width:
        previous = partial_sums[length]
        partial_sums[2 * length] = previous[:, :, :-length] + previous[:, :, length:]
        length = 2 * length
    total = None
    begin = 0
    remain = width
    while remain > 0:
        if length <= remain:
            piece = partial_sums[length][:, :, begin : begin + samples]
            total = piece if total is None else total + piece
            begin = begin + length
            remain = remain - length
        length = length // 2
    return total


def normal_terms(resid_four, conf_four, table):
    row_count = resid_four.shape[0]
    windows = resid_four.shape[2]
    crossl = resid_four.shape[1]
    grad = jnp.einsum(
        "ixwu,wku->ikwx", conf_four * resid_four, table, precision=lax.Precision.HIGHEST
    )
    hess = jnp.einsum(
        "ixwu,wku,wju->ikjwx", conf_four, table, table, precision=lax.Precision.HIGHEST
    )
    return jnp.concatenate([grad, hess.reshape(row_count, KW * KW, windows, crossl)], axis=1)


def per_device(baseline, monitor, shift_model, knot_start, half_width):
    inline_rows = baseline.shape[0]
    slab_width = baseline.shape[1]
    samples = baseline.shape[2]
    paired = extended(jnp.stack([baseline, monitor]), (("xl", 2),), HMAX)
    base_ext = paired[0]
    moni_ext = paired[1]
    half_span = half_width[0]
    lateral = [
        (jnp.abs(offset) <= half_span).astype(jnp.float32) for offset in range(-HMAX, HMAX + 1)
    ]

    def smooth(values):
        timed = box_time(values)
        total = None
        for place, offset in enumerate(range(-HMAX, HMAX + 1)):
            term = lateral[place] * timed[:, HMAX + offset : HMAX + offset + slab_width]
            total = term if total is None else total + term
        return total

    energy_base = smooth(base_ext * base_ext)
    moni_pad = jnp.pad(moni_ext, ((0, 0), (0, 0), (LAGS, LAGS)))
    energy_mon = smooth(moni_pad * moni_pad)

    def one_lag(lag_index, running):
        total_exp, total_shift, total_corr = running
        lagged = lax.dynamic_slice_in_dim(moni_pad, lag_index, samples, 2)
        correlation = smooth(base_ext * lagged)
        energy = lax.dynamic_slice_in_dim(energy_mon, lag_index, samples, 2)
        normed = correlation / jnp.sqrt(energy_base * energy + EPSILON)
        weight_exp = jnp.exp(SHARPNESS * normed)
        lag_value = jnp.asarray(lag_index - LAGS, jnp.int32).astype(jnp.float32)
        return (
            total_exp + weight_exp,
            total_shift + lag_value * weight_exp,
            total_corr + normed * weight_exp,
        )

    first_lag = one_lag(0, (0.0 * energy_base, 0.0 * energy_base, 0.0 * energy_base))
    total_exp, total_shift, total_corr = lax.fori_loop(1, 2 * LAGS + 1, one_lag, first_lag)
    shift_obs = total_shift / total_exp
    confidence = 0.5 + 0.5 * total_corr / total_exp
    table = basis_table(knot_start)
    modelled = jnp.einsum(
        "kwx,wku->xwu", shift_model, table, precision=lax.Precision.HIGHEST
    ).reshape(slab_width, samples)
    resid = shift_obs - modelled[None]
    resid_piece = lax.all_to_all(resid, "xl", split_axis=2, concat_axis=1, tiled=True)
    conf_piece = lax.all_to_all(confidence, "xl", split_axis=2, concat_axis=1, tiled=True)
    row_count = resid_piece.shape[0]
    crossl = resid_piece.shape[1]
    owned = resid_piece.shape[2] // WINLEN
    table_own = lax.dynamic_slice_in_dim(table, lax.axis_index("xl") * owned, owned, 0)
    resid_four = resid_piece.reshape(row_count, crossl, owned, WINLEN)
    conf_four = conf_piece.reshape(row_count, crossl, owned, WINLEN)
    per_row = normal_terms(resid_four, conf_four, table_own)
    normal = jnp.sum(per_row, axis=0)
    summed = lax.psum(normal, "inl")
    share = summed.shape[2] // lax.axis_size("inl")
    summed = lax.dynamic_slice_in_dim(summed, lax.axis_index("inl") * share, share, 2)
    damping = DAMPING * inline_rows * lax.axis_size("inl")
    matrix = [
        [
            summed[KW + KW * first_k + second_k] + (damping if first_k == second_k else 0.0)
            for second_k in range(KW)
        ]
        for first_k in range(KW)
    ]
    target = [summed[first_k] for first_k in range(KW)]
    delta = solve_small(matrix, target)
    return (shift_obs, delta)


def solution(mesh):
    in_specs = (P("inl", "xl", None), P("inl", "xl", None), P(None, None, "xl"), P(), P("xl"))
    out_specs = (P("inl", "xl", None), P(None, "xl", "inl"))
    return jax.shard_map(
        per_device, mesh=mesh, in_specs=in_specs, out_specs=out_specs, check_vma=False
    )
```

profile of v0, /device:TPU:0, one launch (start us, length us, event | category | flops | bytes accessed | tf_op | source)
XLA Modules:
  0.0 127.3 jit_solution(12901075774814896960)
XLA Ops:
  0.6 1.2 pad_maximum_fusion.2
  1.9 1.3 %collective-permute-start.1 = (f32[2,4,3,1024]{3,2,1,0:T(4,128)S(1)}, f32[2,4,3,1024]{3,2,1,0:T(4,128)S(1)}, u32[]{:S(2)}, u32[]{:S(2)}) collective-permute-start(f32[2,4,3,1024]{3,2,1,0:T(4,128)S(1)} %get-tuple-element.489), channel_id=1, source_target_pairs={{1,0},{2,1},{3,2},{4,3},{5,4},{6,5},{7,6},{9,8},{10,9},{11,10},{12... | collective-permute-start | bytes 294920 | tf_op jit(solution)/shard_map/ppermute | solution.py:25
  3.2 5.5 %collective-permute-start = (f32[2,4,3,1024]{3,2,1,0:T(4,128)S(1)}, f32[2,4,3,1024]{3,2,1,0:T(4,128)S(1)}, u32[]{:S(2)}, u32[]{:S(2)}) collective-permute-start(f32[2,4,3,1024]{3,2,1,0:T(4,128)S(1)} %get-tuple-element.488), channel_id=1, source_target_pairs={{0,1},{1,2},{2,3},{3,4},{4,5},{5,6},{6,7},{8,9},{9,10},{10,11},{11... | collective-permute-start | bytes 294920 | tf_op jit(solution)/shard_map/ppermute | solution.py:22
  8.7 0.8 copy.41
  9.5 0.7 convert_element_type.72
  10.3 0.8 convolution_bitcast_fusion
  12.0 1.2 collective-permute-done
  14.6 0.5 slice_add_fusion.14
  17.4 0.5 multiply_add_fusion.2
  18.0 56.6 %while.21 = (s32[]{:T(128)}, f32[4,16,1024]{2,1,0:T(8,128)S(1)}, f32[4,16,1024]{2,1,0:T(8,128)S(1)}, f32[4,16,1024]{2,1,0:T(8,128)S(1)}, f32[]{:T(128)}, /*index...) while((s32[]{:T(128)}, f32[4,16,1024]{2,1,0:T(8,128)S(1)}, ...), condition=%wide.region_1.2_spmd, body=%wide.region_0.1_spmd.sunk | while | flops 2143487 | bytes 11726543 | solution.py:153
  74.6 1.7 %copy.36 = f32[4,16,1024]{1,0,2:T(4,128)} copy(f32[4,16,1024]{2,1,0:T(8,128)S(1)} %get-tuple-element.429) | data formatting | bytes 524288 | tf_op jit(solution)/shard_map/while | solution.py:153
  76.3 1.7 %copy.37 = f32[4,16,1024]{1,0,2:T(4,128)} copy(f32[4,16,1024]{2,1,0:T(8,128)S(1)} %get-tuple-element.430) | data formatting | bytes 524288 | tf_op jit(solution)/shard_map/while | solution.py:153
  78.1 0.8 copy.39
  78.9 2.3 %reshape.48 = f32[8,1,8192]{2,1,0:T(1,128)} reshape(f32[1024,4,16]{2,1,0:T(4,128)S(1)} %bitcast.52) | data formatting | bytes 524288
  81.2 6.1 %all-to-all-start = ((f32[8,1,8192]{2,1,0:T(1,128)}), f32[8,1,8192]{2,1,0:T(1,128)S(1)}, u32[]{:S(2)}, u32[]{:S(2)}) async-start(f32[8,1,8192]{2,1,0:T(1,128)} %reshape.48), calls=%async_computation | async-start | bytes 524288 | tf_op jit(solution)/shard_map/all_to_all | solution.py:162
  87.3 4.4 %broadcast_subtract_fusion = (f32[4,16,1024]{1,0,2:T(4,128)}, f32[4,16,1024]{1,0,2:T(4,128)S(1)}) fusion(f32[16,1024]{0,1:T(8,128)S(1)} %bitcast.55, f32[4,16,1024]{1,0,2:T(4,128)} %copy.36, f32[4,16,1024]{1,0,2:T(4,128)} %copy.37), kind=kLoop, calls=%fused_computation.31 | loop fusion | flops 131072 | bytes 1114112 | tf_op jit(solution)/shard_map/sub | solution.py:160
  91.7 3.8 %reshape.50 = f32[8,1,8192]{2,1,0:T(1,128)} reshape(f32[1024,4,16]{2,1,0:T(4,128)} %bitcast.51) | data formatting | bytes 524288
  95.5 0.6 all-to-all-done
  96.1 5.4 %all-to-all-start.1 = ((f32[8,1,8192]{2,1,0:T(1,128)}), f32[8,1,8192]{2,1,0:T(1,128)S(1)}, u32[]{:S(2)}, u32[]{:S(2)}) async-start(f32[8,1,8192]{2,1,0:T(1,128)} %reshape.50), calls=%async_computation.1 | async-start | bytes 524288 | tf_op jit(solution)/shard_map/all_to_all | solution.py:161
  101.7 1.4 %copy.50 = f32[4,16,1024]{2,1,0:T(8,128)} copy(f32[4,16,1024]{1,0,2:T(4,128)S(1)} %get-tuple-element.474) | data formatting | bytes 524288
  103.2 0.5 broadcast.174
  103.7 1.3 reduce
  105.0 1.5 %reshape.49 = f32[1024,4,16]{2,1,0:T(4,128)S(1)} reshape(f32[8,8192]{1,0:T(8,128)S(1)} %reduce) | data formatting | bytes 524288
  106.5 0.8 copy.40
  107.7 1.0 convolution_bitcast_fusion.1
  108.7 1.1 all-to-all-done.1
  109.9 1.3 reduce.1
  111.1 1.5 %reshape.51 = f32[1024,4,16]{2,1,0:T(4,128)S(1)} reshape(f32[8,8192]{1,0:T(8,128)S(1)} %reduce.1) | data formatting | bytes 524288
  112.7 0.8 copy.44
  114.2 1.6 %convolution_bitcast_fusion.2 = f32[4,4,4,128]{3,1,0,2:T(4,128)S(1)} fusion(f32[4,128,4,32]{3,2,1,0:T(4,128)S(1)} %mul.591, f32[32,4,32]{2,1,0:T(4,128)} %copy-done.2, s32[]{:T(128)S(6)} %select_n.40), kind=kOutput, calls=%fused_computation.28 | convolution fusion | flops 3145728 | bytes 303108 | tf_op jit(solution)/shard_map/ixwu,wku->ikwx/dot_general | solution.py:105
  115.9 10.5 %psum.7 = f32[20,4,128]{2,1,0:T(4,128)S(1)} all-reduce(f32[20,4,128]{2,1,0:T(4,128)S(1)} %copy.49), channel_id=1, replica_groups=mesh['inl'=4,'xl'=8] {'inl'}, use_global_device_ids=true, to_apply=%region_3.4 | all-reduce | flops 10240 | bytes 81920 | tf_op jit(solution)/shard_map/psum | solution.py:171
  126.7 0.6 pad_maximum_fusion.3
  (281 shorter events, 60.4 us)
Async XLA Ops:
  0.6 12.6 %copy-start = (f32[4,16,1024]{2,1,0:T(8,128)S(1)}, f32[4,16,1024]{2,1,0:T(8,128)}, u32[]{:S(2)}) copy-start(f32[4,16,1024]{2,1,0:T(8,128)} %param.8) | copy-start | bytes 786436
  0.6 12.6 %copy-start.1 = (f32[4,16,1024]{2,1,0:T(8,128)S(1)}, f32[4,16,1024]{2,1,0:T(8,128)}, u32[]{:S(2)}) copy-start(f32[4,16,1024]{2,1,0:T(8,128)} %param.7) | copy-start | bytes 786436
  1.9 10.1 %collective-permute-start.1 = (f32[2,4,3,1024]{3,2,1,0:T(4,128)S(1)}, f32[2,4,3,1024]{3,2,1,0:T(4,128)S(1)}, u32[]{:S(2)}, u32[]{:S(2)}) collective-permute-start(f32[2,4,3,1024]{3,2,1,0:T(4,128)S(1)} %get-tuple-element.489), channel_id=1, source_target_pairs={{1,0},{2,1},{3,2},{4,3},{5,4},{6,5},{7,6},{9,8},{10,9},{11,10},{12... | collective-permute-start | bytes 294920 | tf_op jit(solution)/shard_map/ppermute | solution.py:25
  3.2 10.0 %collective-permute-start = (f32[2,4,3,1024]{3,2,1,0:T(4,128)S(1)}, f32[2,4,3,1024]{3,2,1,0:T(4,128)S(1)}, u32[]{:S(2)}, u32[]{:S(2)}) collective-permute-start(f32[2,4,3,1024]{3,2,1,0:T(4,128)S(1)} %get-tuple-element.488), channel_id=1, source_target_pairs={{0,1},{1,2},{2,3},{3,4},{4,5},{5,6},{6,7},{8,9},{9,10},{10,11},{11... | collective-permute-start | bytes 294920 | tf_op jit(solution)/shard_map/ppermute | solution.py:22
  81.2 14.9 %all-to-all-start = ((f32[8,1,8192]{2,1,0:T(1,128)}), f32[8,1,8192]{2,1,0:T(1,128)S(1)}, u32[]{:S(2)}, u32[]{:S(2)}) async-start(f32[8,1,8192]{2,1,0:T(1,128)} %reshape.48), calls=%async_computation | async-start | bytes 524288 | tf_op jit(solution)/shard_map/all_to_all | solution.py:162
  96.1 13.8 %all-to-all-start.1 = ((f32[8,1,8192]{2,1,0:T(1,128)}), f32[8,1,8192]{2,1,0:T(1,128)S(1)}, u32[]{:S(2)}, u32[]{:S(2)}) async-start(f32[8,1,8192]{2,1,0:T(1,128)} %reshape.50), calls=%async_computation.1 | async-start | bytes 524288 | tf_op jit(solution)/shard_map/all_to_all | solution.py:161
  101.7 1.5 %copy-start.2 = (f32[32,4,32]{2,1,0:T(4,128)}, f32[32,4,32]{2,1,0:T(4,128)S(1)}, u32[]{:S(2)}) copy-start(f32[32,4,32]{2,1,0:T(4,128)S(1)} %fusion.46) | copy-start | bytes 49156
where the time goes:
time: 128 us; the launch traced here: 127 us
  other arithmetic  63.6 us (50%)
  local copies, waits for them, and re-layouts  24.9 us (19%)
  starting transfers between devices  18.3 us (14%)
  blocking collectives  10.5 us (8%)
  matrix products  3.41 us (3%)
  waiting for transfers between devices  2.93 us (2%)
  loops' own time  2.02 us (2%)
  between operations  1.66 us (1%)
    add x98, other arithmetic, box_time(): previous[:, :, :-length] + previous[:, :, length:]  21.5 us
    add x31, other arithmetic, one_lag(): total_corr + normed * weight_exp  12 us
    unnamed x12, local copies, waits for them, and re-layouts  11.3 us
    psum x1, blocking collectives, per_device(): summed = lax.psum(normal, 'inl')  10.5 us
    add x33, other arithmetic, box_time(): total = piece if total is None else total + piece  9.07 us
    all_to_all x1, starting transfers between devices, per_device(): lax.all_to_all(confidence, 'xl', split_axis=2, concat_axis=1, tiled=True)  6.08 us
    slice x33, local copies, waits for them, and re-layouts, box_time(): previous[:, :, :-length] + previous[:, :, length:]  5.94 us
    ppermute x1, starting transfers between devices, extended(): lax.ppermute(lax.slice_in_dim(block, block.shape[dim] - width, None, axis...  5.51 us
  transfers between devices with their start and end apart: 4, of which 3 were waited for; matrix products, arithmetic and copies ran while one was open for 14% of the time, Pallas kernels for 0%

commit v1 on v0

--- a/solution.py
+++ b/solution.py
@@ -158,7 +158,15 @@
         "kwx,wku->xwu", shift_model, table, precision=lax.Precision.HIGHEST
     ).reshape(slab_width, samples)
     resid = shift_obs - modelled[None]
-    resid_piece = lax.all_to_all(resid, "xl", split_axis=2, concat_axis=1, tiled=True)
+    resid_piece = jnp.concatenate(
+        jax.lax.all_to_all(
+            jnp.stack(jnp.split(resid, jax.lax.axis_size("xl"), axis=2)),
+            "xl",
+            split_axis=0,
+            concat_axis=0,
+        ),
+        axis=1,
+    )
     conf_piece = lax.all_to_all(confidence, "xl", split_axis=2, concat_axis=1, tiled=True)
     row_count = resid_piece.shape[0]
     crossl = resid_piece.shape[1]

time: 128 us -> 125 us (0.977)
  waiting for transfers between devices: 2.93 us -> 14.7 us
  local copies, waits for them, and re-layouts: 24.9 us -> 18.9 us
  other arithmetic: 63.6 us -> 58.7 us
  starting transfers between devices: 18.3 us -> 15.5 us
    all_to_all x1, waiting for transfers between devices: 0.61 us -> 7.35 us  [per_device(): lax.all_to_all(confidence, 'xl', split_axis=2, concat_axis=1, tiled=True)]
    all_to_all x1, waiting for transfers between devices: 1.15 us -> 5.13 us  [per_device(): jax.lax.all_to_all(jnp.stack(jnp.split(resid, jax.lax.axis_size('xl'), ax...]
    sub x1, other arithmetic: 4.44 us -> 0.81 us  [per_device(): resid = shift_obs - modelled[None]]
    while x2 -> x0, local copies, waits for them, and re-layouts: 3.44 us -> none  [per_device(): lax.fori_loop(1, 2 * LAGS + 1, one_lag, first_lag)]
    all_to_all x1, starting transfers between devices: 6.08 us -> 3.59 us  [per_device(): lax.all_to_all(confidence, 'xl', split_axis=2, concat_axis=1, tiled=True)]
    unnamed x12 -> x14, local copies, waits for them, and re-layouts: 11.3 us -> 8.86 us
    ppermute x1, waiting for transfers between devices: 0.01 us -> 2.22 us  [extended(): lax.ppermute(lax.slice_in_dim(block, 0, width, axis=dim), axis, backward)]
  transfers between devices with their start and end apart: 4 -> 4, of which waited for: 3 -> 3; matrix products, arithmetic and copies ran while one was open for 14% -> 5% of each run, Pallas kernels for 0% -> 0%
where the time goes in v1:
time: 125 us
  other arithmetic  58.7 us (47%)
  local copies, waits for them, and re-layouts  18.9 us (15%)
  starting transfers between devices  15.5 us (12%)
  waiting for transfers between devices  14.7 us (12%)
  blocking collectives  10.5 us (8%)
  matrix products  2.73 us (2%)
  loops' own time  2.02 us (2%)
  between operations  1.63 us (1%)
    add x98, other arithmetic, box_time(): previous[:, :, :-length] + previous[:, :, length:]  21.5 us
    add x31, other arithmetic, one_lag(): total_corr + normed * weight_exp  12 us
    psum x1, blocking collectives, per_device(): summed = lax.psum(normal, 'inl')  10.5 us
    add x33, other arithmetic, box_time(): total = piece if total is None else total + piece  9.07 us
    unnamed x14, local copies, waits for them, and re-layouts  8.86 us
    all_to_all x1, waiting for transfers between devices, per_device(): lax.all_to_all(confidence, 'xl', split_axis=2, concat_axis=1, tiled=True)  7.35 us
    slice x33, local copies, waits for them, and re-layouts, box_time(): previous[:, :, :-length] + previous[:, :, length:]  5.94 us
    all_to_all x1, starting transfers between devices, per_device(): jax.lax.all_to_all(jnp.stack(jnp.split(resid, jax.lax.axis_size('xl'), ax...  5.72 us
  transfers between devices with their start and end apart: 4, of which 3 were waited for; matrix products, arithmetic and copies ran while one was open for 5% of the time, Pallas kernels for 0%

profile of v1, /device:TPU:0, one launch (start us, length us, event | category | flops | bytes accessed | tf_op | source)
XLA Modules:
  0.0 124.6 jit_solution(12045519015552787543)
XLA Ops:
  0.6 1.2 pad_maximum_fusion.2
  1.9 4.9 %collective-permute-start = (f32[2,4,3,1024]{3,2,1,0:T(4,128)S(1)}, f32[2,4,3,1024]{3,2,1,0:T(4,128)S(1)}, u32[]{:S(2)}, u32[]{:S(2)}) collective-permute-start(f32[2,4,3,1024]{3,2,1,0:T(4,128)S(1)} %get-tuple-element.486), channel_id=1, source_target_pairs={{0,1},{1,2},{2,3},{3,4},{4,5},{5,6},{6,7},{8,9},{9,10},{10,11},{11... | collective-permute-start | bytes 294920 | tf_op jit(solution)/shard_map/ppermute | solution.py:22
  6.7 1.3 %collective-permute-start.1 = (f32[2,4,3,1024]{3,2,1,0:T(4,128)S(1)}, f32[2,4,3,1024]{3,2,1,0:T(4,128)S(1)}, u32[]{:S(2)}, u32[]{:S(2)}) collective-permute-start(f32[2,4,3,1024]{3,2,1,0:T(4,128)S(1)} %get-tuple-element.487), channel_id=1, source_target_pairs={{1,0},{2,1},{3,2},{4,3},{5,4},{6,5},{7,6},{9,8},{10,9},{11,10},{12... | collective-permute-start | bytes 294920 | tf_op jit(solution)/shard_map/ppermute | solution.py:25
  8.1 0.7 convert_element_type.72
  8.8 0.8 copy.35
  9.7 0.8 convolution_bitcast_fusion
  11.4 2.2 %collective-permute-done.1 = f32[2,4,3,1024]{3,2,1,0:T(4,128)S(1)} collective-permute-done((f32[2,4,3,1024]{3,2,1,0:T(4,128)S(1)}, f32[2,4,3,1024]{3,2,1,0:T(4,128)S(1)}, u32[]{:S(2)}, u32[]{:S(2)}) %collective-permute-start.1) | collective-permute-done | bytes 98336 | tf_op jit(solution)/shard_map/ppermute | solution.py:25
  14.2 0.5 slice_add_fusion.14
  17.8 0.5 multiply_add_fusion.2
  18.4 56.6 %while.21 = (s32[]{:T(128)}, f32[4,16,1024]{2,1,0:T(8,128)S(1)}, f32[4,16,1024]{2,1,0:T(8,128)S(1)}, f32[4,16,1024]{2,1,0:T(8,128)S(1)}, f32[]{:T(128)}, /*index...) while((s32[]{:T(128)}, f32[4,16,1024]{2,1,0:T(8,128)S(1)}, ...), condition=%wide.region_1.2_spmd, body=%wide.region_0.1_spmd.sunk | while | flops 2143487 | bytes 11726543 | solution.py:153
  75.0 0.8 broadcast_subtract_fusion
  75.8 0.6 fusion.67
  76.4 0.6 fusion.66
  77.0 0.6 fusion.65
  77.7 0.6 fusion.64
  78.3 0.6 fusion.63
  78.9 0.6 fusion.62
  79.5 0.6 fusion.61
  80.1 0.6 fusion.60
  80.7 5.7 %all-to-all-start.1 = ((f32[8,4,16,128]{3,2,1,0:T(8,128)}), f32[8,4,16,128]{3,2,1,0:T(8,128)S(1)}, u32[]{:S(2)}, u32[]{:S(2)}) async-start(f32[8,4,16,128]{3,2,1,0:T(8,128)} %fusion.60), calls=%async_computation.1 | async-start | bytes 524288 | tf_op jit(solution)/shard_map/all_to_all | solution.py:162
  86.4 0.8 copy.33
  87.2 2.3 %reshape.47 = f32[8,1,8192]{2,1,0:T(1,128)} reshape(f32[1024,4,16]{2,1,0:T(4,128)S(1)} %bitcast.79) | data formatting | bytes 524288
  89.5 5.1 %all-to-all-done.1 = f32[8,4,16,128]{3,2,1,0:T(8,128)S(1)} async-done(((f32[8,4,16,128]{3,2,1,0:T(8,128)}), f32[8,4,16,128]{3,2,1,0:T(8,128)S(1)}, u32[]{:S(2)}, u32[]{:S(2)}) %all-to-all-start.1) | async-done | bytes 262176 | tf_op jit(solution)/shard_map/all_to_all | solution.py:162
  94.6 3.6 %all-to-all-start = ((f32[8,1,8192]{2,1,0:T(1,128)}), f32[8,1,8192]{2,1,0:T(1,128)S(1)}, u32[]{:S(2)}, u32[]{:S(2)}) async-start(f32[8,1,8192]{2,1,0:T(1,128)} %reshape.47), calls=%async_computation | async-start | bytes 524288 | tf_op jit(solution)/shard_map/all_to_all | solution.py:170
  98.9 7.3 %all-to-all-done = f32[8,1,8192]{2,1,0:T(1,128)S(1)} async-done(((f32[8,1,8192]{2,1,0:T(1,128)}), f32[8,1,8192]{2,1,0:T(1,128)S(1)}, u32[]{:S(2)}, u32[]{:S(2)}) %all-to-all-start) | async-done | bytes 262176 | tf_op jit(solution)/shard_map/all_to_all | solution.py:170
  106.8 1.3 %reduce = f32[8,8192]{1,0:T(8,128)S(1)} reduce(f32[8,1,8192]{2,1,0:T(1,128)S(1)} %all-to-all-done, f32[]{:T(128)} %broadcast.174), dimensions={1}, to_apply=%all_to_all.14.reduce_sub_computation | reduce | bytes 524292 | tf_op jit(solution)/shard_map/all_to_all | solution.py:170
  108.1 1.5 %reshape.48 = f32[1024,4,16]{2,1,0:T(4,128)S(1)} reshape(f32[8,8192]{1,0:T(8,128)S(1)} %reduce) | data formatting | bytes 524288
  109.6 0.8 copy.34
  111.1 0.9 convolution_bitcast_fusion.2
  112.0 1.0 convolution_bitcast_fusion.1
  113.1 10.5 %psum.7 = f32[20,4,128]{2,1,0:T(4,128)S(1)} all-reduce(f32[20,4,128]{2,1,0:T(4,128)S(1)} %copy.42), channel_id=1, replica_groups=mesh['inl'=4,'xl'=8] {'inl'}, use_global_device_ids=true, to_apply=%region_3.4 | all-reduce | flops 10240 | bytes 81920 | tf_op jit(solution)/shard_map/psum | solution.py:179
  124.0 0.6 pad_maximum_fusion.3
  (281 shorter events, 60.9 us)
Async XLA Ops:
  0.6 13.0 %copy-start.1 = (f32[4,16,1024]{2,1,0:T(8,128)S(1)}, f32[4,16,1024]{2,1,0:T(8,128)}, u32[]{:S(2)}) copy-start(f32[4,16,1024]{2,1,0:T(8,128)} %param.7) | copy-start | bytes 786436
  0.6 13.0 %copy-start = (f32[4,16,1024]{2,1,0:T(8,128)S(1)}, f32[4,16,1024]{2,1,0:T(8,128)}, u32[]{:S(2)}) copy-start(f32[4,16,1024]{2,1,0:T(8,128)} %param.8) | copy-start | bytes 786436
  1.9 9.5 %collective-permute-start = (f32[2,4,3,1024]{3,2,1,0:T(4,128)S(1)}, f32[2,4,3,1024]{3,2,1,0:T(4,128)S(1)}, u32[]{:S(2)}, u32[]{:S(2)}) collective-permute-start(f32[2,4,3,1024]{3,2,1,0:T(4,128)S(1)} %get-tuple-element.486), channel_id=1, source_target_pairs={{0,1},{1,2},{2,3},{3,4},{4,5},{5,6},{6,7},{8,9},{9,10},{10,11},{11... | collective-permute-start | bytes 294920 | tf_op jit(solution)/shard_map/ppermute | solution.py:22
  6.7 6.9 %collective-permute-start.1 = (f32[2,4,3,1024]{3,2,1,0:T(4,128)S(1)}, f32[2,4,3,1024]{3,2,1,0:T(4,128)S(1)}, u32[]{:S(2)}, u32[]{:S(2)}) collective-permute-start(f32[2,4,3,1024]{3,2,1,0:T(4,128)S(1)} %get-tuple-element.487), channel_id=1, source_target_pairs={{1,0},{2,1},{3,2},{4,3},{5,4},{6,5},{7,6},{9,8},{10,9},{11,10},{12... | collective-permute-start | bytes 294920 | tf_op jit(solution)/shard_map/ppermute | solution.py:25
  80.7 13.9 %all-to-all-start.1 = ((f32[8,4,16,128]{3,2,1,0:T(8,128)}), f32[8,4,16,128]{3,2,1,0:T(8,128)S(1)}, u32[]{:S(2)}, u32[]{:S(2)}) async-start(f32[8,4,16,128]{3,2,1,0:T(8,128)} %fusion.60), calls=%async_computation.1 | async-start | bytes 524288 | tf_op jit(solution)/shard_map/all_to_all | solution.py:162
  94.6 11.7 %all-to-all-start = ((f32[8,1,8192]{2,1,0:T(1,128)}), f32[8,1,8192]{2,1,0:T(1,128)S(1)}, u32[]{:S(2)}, u32[]{:S(2)}) async-start(f32[8,1,8192]{2,1,0:T(1,128)} %reshape.47), calls=%async_computation | async-start | bytes 524288 | tf_op jit(solution)/shard_map/all_to_all | solution.py:170
